TPU v7x, 32 devices: a whole 2x2x4 slice. The times are simulated.
32 devices in a mesh: dp: 4 (over x, core), seq: 2 (over y), tensor: 4 (over z).
Axes of the slice: x: 2, y: 2, z: 4, core: 2. Of those that a mesh axis runs over, the one named last changes fastest.
Arguments:
- tokens: bfloat16 [8, 1024, 768], P('dp', 'seq'), may hold values from -6 to 6
- segments: int32 [8, 1024], P('dp'), may hold values from 0 to 2, never falling along the last dimension, each value on 1 to 512 neighbouring positions
- projections: bfloat16 [3, 768, 768], P(None, ('dp', 'seq'), 'tensor'), may hold values from -0.21875 to 0.21875
- offsets: bfloat16 [2, 12, 64], P(None, 'tensor', ('dp', 'seq')), may hold values from -3 to 3
- mixing: bfloat16 [768, 768], P('tensor', ('dp', 'seq')), may hold values from -2.5 to 2.5
- upward: bfloat16 [768, 3072], P(('dp', 'seq'), 'tensor'), may hold values from -0.21875 to 0.21875
- thresholds: bfloat16 [48, 64], P('tensor', ('dp', 'seq')), may hold values from -3 to 3
- downward: bfloat16 [3072, 768], P('tensor', ('dp', 'seq')), may hold values from -0.109375 to 0.109375
- scales: bfloat16 [2, 768], P(None, ('dp', 'seq')), may hold values from 0.099609375 to 1.8984375
- shifts: bfloat16 [2, 768], P(None, ('dp', 'seq')), may hold values from -2 to 2
- biases: bfloat16 [2, 768], P(None, ('dp', 'seq')), may hold values from -2 to 2
- cotangent: bfloat16 [8, 1024, 768], P('dp', 'seq'), may hold values from -6 to 6
Outputs:
- result: bfloat16 [8, 1024, 768], P('dp', 'seq')
- tokens_grad: bfloat16 [8, 1024, 768], P('dp', 'seq')
- projections_grad: float32 [3, 768, 768], P(None, ('dp', 'seq'), 'tensor')
- offsets_grad: float32 [2, 12, 64], P(None, 'tensor', ('dp', 'seq'))
- mixing_grad: float32 [768, 768], P('tensor', ('dp', 'seq'))
- upward_grad: float32 [768, 3072], P(('dp', 'seq'), 'tensor')
- thresholds_grad: float32 [48, 64], P('tensor', ('dp', 'seq'))
- downward_grad: float32 [3072, 768], P('tensor', ('dp', 'seq'))
- scales_grad: float32 [2, 768], P(None, ('dp', 'seq'))
- shifts_grad: float32 [2, 768], P(None, ('dp', 'seq'))
- biases_grad: float32 [2, 768], P(None, ('dp', 'seq'))
Inputs may be any that keep to these rules, and one draw needn't show every extreme that they name: `segments`: ids never fall along a sequence; each document holds 1 to 512 tokens, and one holds exactly 512.
All inputs are finite; a program needn't handle non-finite values.
Results may differ from a plain program's by a relative error of at most 0.012.
Values may be sent and summed in bfloat16 or wider, within the bound.
A program may use at most 128 MiB of HBM per device.

v0:
```python
import jax
import jax.numpy as jnp
from jax import lax
from jax.sharding import PartitionSpec as P


def norm_rows(values, gain_row, shift_row):
    average = jnp.mean(values, axis=-1, keepdims=True)
    centered = values - average
    variance = jnp.mean(centered * centered, axis=-1, keepdims=True)
    return centered * lax.rsqrt(variance + 1e-05) * gain_row + shift_row


def gelu_tanh(values):
    return (
        0.5
        * values
        * (1.0 + jnp.tanh(0.7978845608028654 * (values + 0.044715 * values * values * values)))
    )


def head_scores(query_head, key_head, allowed):
    scores = (
        jnp.einsum("qe,ke->qk", query_head, key_head, preferred_element_type=jnp.float32) * 0.125
    )
    return jnp.where(allowed, scores, -1e30)


def accumulate(running, addition):
    return addition if running is None else running + addition


def per_device(
    tokens,
    segments,
    projections,
    offsets,
    mixing,
    upward,
    thresholds,
    downward,
    scales,
    shifts,
    biases,
    cotangent,
):
    micro = tokens.shape[0]
    block_len = tokens.shape[1]
    seq_len = segments.shape[1]
    head_size = offsets.shape[2] * lax.axis_size(("dp", "seq"))
    start = lax.axis_index("seq") * block_len
    query_pos = start + jnp.arange(block_len, dtype=jnp.int32)
    key_pos = jnp.arange(seq_len, dtype=jnp.int32)
    saved = []
    results = []
    for batch_index in range(micro):
        gathered = (
            lax.all_gather(projections, ("dp", "seq"), axis=1, tiled=True),
            lax.all_gather(offsets, ("dp", "seq"), axis=2, tiled=True),
            lax.all_gather(mixing, ("dp", "seq"), axis=1, tiled=True),
            lax.all_gather(upward, ("dp", "seq"), axis=0, tiled=True),
            lax.all_gather(thresholds, ("dp", "seq"), axis=1, tiled=True),
            lax.all_gather(downward, ("dp", "seq"), axis=1, tiled=True),
            lax.all_gather(scales, ("dp", "seq"), axis=1, tiled=True),
            lax.all_gather(shifts, ("dp", "seq"), axis=1, tiled=True),
            lax.all_gather(biases, ("dp", "seq"), axis=1, tiled=True),
        )
        (
            entry_weights,
            entry_offsets,
            mixer_weights,
            upward_full,
            threshold_full,
            downward_full,
            scale_full,
            shift_full,
            biases_full,
        ) = gathered
        scale_rows = scale_full.astype(jnp.float32)
        shift_rows = shift_full.astype(jnp.float32)
        bias_rows = biases_full.astype(jnp.float32)
        offset_rows = entry_offsets.astype(jnp.float32).reshape(2, -1)
        inputs = tokens[batch_index].astype(jnp.float32)
        normed = norm_rows(inputs, scale_rows[0], shift_rows[0]).astype(jnp.bfloat16)
        stacked = jnp.einsum(
            "cd,tde->tce", normed, entry_weights, preferred_element_type=jnp.float32
        )
        query_b = (stacked[0] + offset_rows[0]).astype(jnp.bfloat16)
        key_b = stacked[1].astype(jnp.bfloat16)
        value_b = (stacked[2] + offset_rows[1]).astype(jnp.bfloat16)
        key_full, value_full = (
            lax.all_gather(key_b, "seq", axis=0, tiled=True),
            lax.all_gather(value_b, "seq", axis=0, tiled=True),
        )
        seg_row = segments[batch_index]
        own_seg = lax.dynamic_slice_in_dim(seg_row, start, block_len)
        allowed = (key_pos[None, :] <= query_pos[:, None]) & (seg_row[None, :] == own_seg[:, None])
        head_count = query_b.shape[1] // head_size
        pieces = []
        totals = []
        for head_index in range(head_count):
            columns = slice(head_index * head_size, (head_index + 1) * head_size)
            scores = head_scores(query_b[:, columns], key_full[:, columns], allowed)
            log_total = jax.nn.logsumexp(scores, axis=1, keepdims=True)
            weights_b = jnp.exp(scores - log_total).astype(jnp.bfloat16)
            pieces.append(
                jnp.dot(weights_b, value_full[:, columns], preferred_element_type=jnp.float32)
            )
            totals.append(log_total)
        attended = jnp.concatenate(pieces, axis=1).astype(jnp.bfloat16)
        branch = lax.psum(
            jnp.dot(attended, mixer_weights, preferred_element_type=jnp.float32), "tensor"
        )
        hidden = inputs + branch + bias_rows[0]
        normed2 = norm_rows(hidden, scale_rows[1], shift_rows[1]).astype(jnp.bfloat16)
        pre_act = jnp.dot(
            normed2, upward_full, preferred_element_type=jnp.float32
        ) + threshold_full.astype(jnp.float32).reshape(-1)
        activated = gelu_tanh(pre_act).astype(jnp.bfloat16)
        lifted = lax.psum(
            jnp.dot(activated, downward_full, preferred_element_type=jnp.float32).astype(
                jnp.bfloat16
            ),
            "tensor",
        ).astype(jnp.float32)
        results.append((hidden + lifted + bias_rows[1]).astype(jnp.bfloat16))
        kept_keys = (key_b, value_b)
        saved.append(
            (
                inputs,
                normed,
                query_b,
                kept_keys,
                allowed,
                totals,
                attended,
                hidden,
                normed2,
                pre_act,
                activated,
            )
        )
    entry_acc = None
    offset_acc = None
    mixer_acc = None
    upward_acc = None
    threshold_acc = None
    downward_acc = None
    scale_acc = None
    shift_acc = None
    bias_acc = None
    input_grads = []
    for batch_index in range(micro):
        gathered = (
            lax.all_gather(projections, ("dp", "seq"), axis=1, tiled=True),
            lax.all_gather(offsets, ("dp", "seq"), axis=2, tiled=True),
            lax.all_gather(mixing, ("dp", "seq"), axis=1, tiled=True),
            lax.all_gather(upward, ("dp", "seq"), axis=0, tiled=True),
            lax.all_gather(thresholds, ("dp", "seq"), axis=1, tiled=True),
            lax.all_gather(downward, ("dp", "seq"), axis=1, tiled=True),
            lax.all_gather(scales, ("dp", "seq"), axis=1, tiled=True),
            lax.all_gather(shifts, ("dp", "seq"), axis=1, tiled=True),
            lax.all_gather(biases, ("dp", "seq"), axis=1, tiled=True),
        )
        (
            entry_weights,
            entry_offsets,
            mixer_weights,
            upward_full,
            threshold_full,
            downward_full,
            scale_full,
            shift_full,
            biases_full,
        ) = gathered
        scale_rows = scale_full.astype(jnp.float32)
        shift_rows = shift_full.astype(jnp.float32)
        (
            inputs,
            normed,
            query_b,
            kept_keys,
            allowed,
            totals,
            attended,
            hidden,
            normed2,
            pre_act,
            activated,
        ) = saved[batch_index]
        grad_out = cotangent[batch_index].astype(jnp.float32)
        grad_out_b = grad_out.astype(jnp.bfloat16)
        downward_acc = accumulate(
            downward_acc,
            jnp.einsum("cf,cd->fd", activated, grad_out_b, preferred_element_type=jnp.float32),
        )
        grad_act = jnp.einsum(
            "cd,fd->cf", grad_out_b, downward_full, preferred_element_type=jnp.float32
        )
        unused, gelu_back = jax.vjp(gelu_tanh, pre_act)
        grad_pre = gelu_back(grad_act)[0].astype(jnp.bfloat16)
        threshold_acc = accumulate(threshold_acc, jnp.sum(grad_pre.astype(jnp.float32), axis=0))
        upward_acc = accumulate(
            upward_acc,
            jnp.einsum("cd,cf->df", normed2, grad_pre, preferred_element_type=jnp.float32),
        )
        grad_normed2 = lax.psum(
            jnp.einsum("cf,df->cd", grad_pre, upward_full, preferred_element_type=jnp.float32),
            "tensor",
        )
        unused, second_back = jax.vjp(norm_rows, hidden, scale_rows[1], shift_rows[1])
        grad_from_norm, scale_second, shift_second = second_back(grad_normed2)
        grad_hidden = grad_out + grad_from_norm
        grad_hidden_b = grad_hidden.astype(jnp.bfloat16)
        mixer_acc = accumulate(
            mixer_acc,
            jnp.einsum("ce,cd->ed", attended, grad_hidden_b, preferred_element_type=jnp.float32),
        )
        grad_attended = jnp.einsum(
            "cd,ed->ce", grad_hidden_b, mixer_weights, preferred_element_type=jnp.float32
        ).astype(jnp.bfloat16)
        own_keys, own_values = kept_keys
        key_full, value_full = (
            lax.all_gather(own_keys, "seq", axis=0, tiled=True),
            lax.all_gather(own_values, "seq", axis=0, tiled=True),
        )
        head_count = query_b.shape[1] // head_size
        query_grads = []
        key_grads = []
        value_grads = []
        for head_index in range(head_count):
            columns = slice(head_index * head_size, (head_index + 1) * head_size)
            scores = head_scores(query_b[:, columns], key_full[:, columns], allowed)
            probs = jnp.exp(scores - totals[head_index])
            grad_slice = grad_attended[:, columns]
            grad_probs = jnp.einsum(
                "qe,ke->qk", grad_slice, value_full[:, columns], preferred_element_type=jnp.float32
            )
            delta_rows = jnp.sum(probs * grad_probs, axis=1, keepdims=True)
            grad_scores = (probs * (grad_probs - delta_rows)).astype(jnp.bfloat16)
            query_grads.append(
                jnp.einsum(
                    "qk,ke->qe",
                    grad_scores,
                    key_full[:, columns],
                    preferred_element_type=jnp.float32,
                )
                * 0.125
            )
            probs_b = probs.astype(jnp.bfloat16)
            value_grads.append(
                jnp.einsum("qk,qe->ke", probs_b, grad_slice, preferred_element_type=jnp.float32)
            )
            key_grads.append(
                jnp.einsum(
                    "qk,qe->ke",
                    grad_scores,
                    query_b[:, columns],
                    preferred_element_type=jnp.float32,
                )
                * 0.125
            )
        key_grad_full = jnp.concatenate(key_grads, axis=1)
        value_grad_full = jnp.concatenate(value_grads, axis=1)
        key_grad, value_grad = (
            lax.psum_scatter(key_grad_full, "seq", scatter_dimension=0, tiled=True),
            lax.psum_scatter(value_grad_full, "seq", scatter_dimension=0, tiled=True),
        )
        triple = jnp.stack([jnp.concatenate(query_grads, axis=1), key_grad, value_grad]).astype(
            jnp.bfloat16
        )
        triple_sums = jnp.sum(triple.astype(jnp.float32), axis=1)
        offset_acc = accumulate(offset_acc, jnp.stack([triple_sums[0], triple_sums[2]]))
        entry_acc = accumulate(
            entry_acc, jnp.einsum("cd,tce->tde", normed, triple, preferred_element_type=jnp.float32)
        )
        grad_normed = lax.psum(
            jnp.einsum("tce,tde->cd", triple, entry_weights, preferred_element_type=jnp.float32),
            "tensor",
        )
        unused, first_back = jax.vjp(norm_rows, inputs, scale_rows[0], shift_rows[0])
        grad_inputs, scale_first, shift_first = first_back(grad_normed)
        input_grads.append((grad_hidden + grad_inputs).astype(jnp.bfloat16))
        scale_acc = accumulate(scale_acc, jnp.stack([scale_first, scale_second]))
        shift_acc = accumulate(shift_acc, jnp.stack([shift_first, shift_second]))
        bias_acc = accumulate(
            bias_acc, jnp.stack([jnp.sum(grad_hidden, axis=0), jnp.sum(grad_out, axis=0)])
        )
    offset_acc = offset_acc.reshape(entry_offsets.shape)
    threshold_acc = threshold_acc.reshape(threshold_full.shape)
    summed = (
        lax.psum_scatter(entry_acc, ("dp", "seq"), scatter_dimension=1, tiled=True),
        lax.psum_scatter(offset_acc, ("dp", "seq"), scatter_dimension=2, tiled=True),
        lax.psum_scatter(mixer_acc, ("dp", "seq"), scatter_dimension=1, tiled=True),
        lax.psum_scatter(upward_acc, ("dp", "seq"), scatter_dimension=0, tiled=True),
        lax.psum_scatter(threshold_acc, ("dp", "seq"), scatter_dimension=1, tiled=True),
        lax.psum_scatter(downward_acc, ("dp", "seq"), scatter_dimension=1, tiled=True),
        lax.psum_scatter(scale_acc, ("dp", "seq"), scatter_dimension=1, tiled=True),
        lax.psum_scatter(shift_acc, ("dp", "seq"), scatter_dimension=1, tiled=True),
        lax.psum_scatter(bias_acc, ("dp", "seq"), scatter_dimension=1, tiled=True),
    )
    return (
        jnp.stack(results),
        jnp.stack(input_grads),
        summed[0],
        summed[1],
        summed[2],
        summed[3],
        summed[4],
        summed[5],
        summed[6],
        summed[7],
        summed[8],
    )


def solution(mesh):
    placed = (
        P("dp", "seq", None),
        P("dp", None),
        P(None, ("dp", "seq"), "tensor"),
        P(None, "tensor", ("dp", "seq")),
        P("tensor", ("dp", "seq")),
        P(("dp", "seq"), "tensor"),
        P("tensor", ("dp", "seq")),
        P("tensor", ("dp", "seq")),
        P(None, ("dp", "seq")),
        P(None, ("dp", "seq")),
        P(None, ("dp", "seq")),
        P("dp", "seq", None),
    )
    return jax.shard_map(
        per_device,
        mesh=mesh,
        in_specs=placed,
        out_specs=(
            P("dp", "seq", None),
            P("dp", "seq", None),
            P(None, ("dp", "seq"), "tensor"),
            P(None, "tensor", ("dp", "seq")),
            P("tensor", ("dp", "seq")),
            P(("dp", "seq"), "tensor"),
            P("tensor", ("dp", "seq")),
            P("tensor", ("dp", "seq")),
            P(None, ("dp", "seq")),
            P(None, ("dp", "seq")),
            P(None, ("dp", "seq")),
        ),
        check_vma=False,
    )
```

profile of v0, /device:TPU:0, one launch (start us, length us, event | category | flops | bytes accessed | tf_op | source)
XLA Modules:
  0.0 897.6 jit_solution(6401317190653829994)
XLA Ops:
  9.0 13.2 %all-gather.2 = bf16[8,96,2]{1,2,0:T(2,128)(2,1)S(1)} all-gather(bf16[1,96,2]{1,2,0:T(2,128)(2,1)} %bitcast.306), channel_id=1, replica_groups=mesh['dp'=4,'seq'=2,'tensor'=4] {'dp','seq'}, dimensions={0}, use_global_device_ids=true | all-gather | bytes 3456 | tf_op jit(solution)/shard_map/all_gather | solution.py:64
  22.3 10.9 %all-gather.3 = bf16[8,96,2]{1,2,0:T(2,128)(2,1)S(1)} all-gather(bf16[1,96,2]{1,2,0:T(2,128)(2,1)} %bitcast.307), channel_id=1, replica_groups=mesh['dp'=4,'seq'=2,'tensor'=4] {'dp','seq'}, dimensions={0}, use_global_device_ids=true | all-gather | bytes 3456 | tf_op jit(solution)/shard_map/all_gather | solution.py:65
  36.2 12.5 %all_gather.29 = bf16[2,3,64]{1,0,2:T(2,128)(2,1)S(1)} all-gather(bf16[2,3,8]{1,0,2:T(2,128)(2,1)S(1)} %copy.73), channel_id=1, replica_groups=mesh['dp'=4,'seq'=2,'tensor'=4] {'dp','seq'}, dimensions={2}, use_global_device_ids=true | all-gather | bytes 864 | tf_op jit(solution)/shard_map/all_gather | solution.py:59
  49.3 23.8 %all_gather.28 = bf16[3,768,192]{2,0,1:T(4,128)(2,1)S(1)} all-gather(bf16[3,96,192]{2,0,1:T(4,128)(2,1)S(1)} %copy.71), channel_id=1, replica_groups=mesh['dp'=4,'seq'=2,'tensor'=4] {'dp','seq'}, dimensions={1}, use_global_device_ids=true | all-gather | bytes 995328 | tf_op jit(solution)/shard_map/all_gather | solution.py:58
  79.8 8.4 all-gather
  96.4 7.5 all-gather.1
  110.1 15.6 %all_gather.32 = bf16[192,768]{0,1:T(8,128)(2,1)S(1)} all-gather(bf16[192,96]{0,1:T(8,128)(2,1)S(1)} %copy.76), channel_id=1, replica_groups=mesh['dp'=4,'seq'=2,'tensor'=4] {'dp','seq'}, dimensions={1}, use_global_device_ids=true | all-gather | bytes 331776 | tf_op jit(solution)/shard_map/all_gather | solution.py:60
  125.8 8.2 all_gather.74
  134.0 8.1 all_gather.31
  159.2 11.3 %all-gather.4 = bf16[8,96,2]{1,2,0:T(2,128)(2,1)S(1)} all-gather(bf16[1,96,2]{1,2,0:T(2,128)(2,1)S(1)} %bitcast.308), channel_id=1, replica_groups=mesh['dp'=4,'seq'=2,'tensor'=4] {'dp','seq'}, dimensions={0}, use_global_device_ids=true | all-gather | bytes 3456 | tf_op jit(solution)/shard_map/all_gather | solution.py:66
  171.3 16.3 %all_gather.35 = bf16[12,64]{0,1:T(8,128)(2,1)S(1)} all-gather(bf16[12,8]{0,1:T(8,128)(2,1)S(1)} %copy-done.131), channel_id=1, replica_groups=mesh['dp'=4,'seq'=2,'tensor'=4] {'dp','seq'}, dimensions={1}, use_global_device_ids=true | all-gather | bytes 1728 | tf_op jit(solution)/shard_map/all_gather | solution.py:62
  188.3 91.5 %all-reduce.16.cloned.1.call-done = (f32[512,768]{1,0:T(8,128)}, f32[512,768]{1,0:T(8,128)}) async-done(((f32[512,768]{1,0:T(8,128)}, f32[512,768]{1,0:T(8,128)}), (f32[512,768]{1,0:T(8,128)}, f32[512,768]{1,0:T(8,128)})) %all-reduce.16.cloned.1.call-update) | async-done | bytes 3145744 | tf_op jit(solution)/shard_map/psum | solution.py:111
  284.5 3.9 convolution_add_fusion.3
  290.6 4.5 convert_reduce_fusion.5
  301.6 3.9 convolution_convert_fusion.1
  307.7 114.4 %all-reduce.14.cloned.1.call-done = (f32[512,768]{1,0:T(8,128)}, f32[512,768]{1,0:T(8,128)}) async-done(((f32[512,768]{1,0:T(8,128)}, f32[512,768]{1,0:T(8,128)}), (f32[512,768]{1,0:T(8,128)}, f32[512,768]{1,0:T(8,128)})) %all-reduce.14.cloned.1.call-update) | async-done | bytes 3145744 | tf_op jit(solution)/shard_map/psum | solution.py:207
  422.1 3.6 multiply_reduce_fusion.6
  426.9 66.1 %all-reduce.18.cloned.1.call-done = (bf16[512,768]{1,0:T(8,128)(2,1)}, bf16[512,768]{1,0:T(8,128)(2,1)}) async-done(((bf16[512,768]{1,0:T(8,128)(2,1)}, bf16[512,768]{1,0:T(8,128)(2,1)}), (bf16[512,768]{1,0:T(8,128)(2,1)}, bf16[512,768]{1,0:T(8,128)(2,1)})) %all-reduce.18.cloned.1.call-update) | async-done | bytes 1572880 | tf_op jit(solution)/shard_map/psum | solution.py:120
  493.1 5.0 fusion.183
  565.5 6.5 reduce-scatter.24.cloned.1.call-done
  577.0 14.7 %reduce-scatter.28.cloned.1.call-done = f32[512,192]{0,1:T(8,128)} async-done(((f32[1024,192]{0,1:T(8,128)}), f32[512,192]{0,1:T(8,128)}) %reduce-scatter.28.cloned.1.call-update) | async-done | bytes 393232 | tf_op jit(solution)/shard_map/reduce_scatter | solution.py:266
  593.3 3.3 convolution_bitcast_fusion
  614.5 4.3 copy.85
  618.8 4.7 reshape.318
  623.7 4.1 fusion.66
  630.1 88.1 %all-reduce.12.cloned.1.call-done = (f32[512,768]{1,0:T(8,128)}, f32[512,768]{1,0:T(8,128)}) async-done(((f32[512,768]{1,0:T(8,128)}, f32[512,768]{1,0:T(8,128)}), (f32[512,768]{1,0:T(8,128)}, f32[512,768]{1,0:T(8,128)})) %all-reduce.12.cloned.1.call-update) | async-done | bytes 3145744 | tf_op jit(solution)/shard_map/psum | solution.py:277
  730.3 4.9 convolution_add_fusion
  752.4 24.1 %all-reduce.2 = (f32[2,3,64]{2,1,0:T(4,128)S(1)}, f32[12,64]{1,0:T(8,128)S(1)}) all-reduce(f32[2,3,64]{2,1,0:T(4,128)S(1)} %maximum_add_fusion.3, f32[12,64]{1,0:T(8,128)} %add.400), channel_id=9, replica_groups=mesh['dp'=4,'seq'=2,'tensor'=4] {'dp','seq'}, use_global_device_ids=true, to_apply=%region_49.50.clone | all-reduce | flops 1152 | bytes 9216
  781.2 3.7 fusion.56
  787.6 9.6 %reduce-scatter.42.cloned.1.call-done = f32[96,2]{1,0:T(8,128)} async-done(((f32[768,2]{1,0:T(8,128)}), f32[96,2]{1,0:T(8,128)}) %reduce-scatter.42.cloned.1.call-update) | async-done | bytes 784
  798.7 45.3 %reduce-scatter.34.cloned.1.call-done = f32[768,96]{0,1:T(8,128)} async-done(((f32[768,768]{0,1:T(8,128)}), f32[768,96]{0,1:T(8,128)}) %reduce-scatter.34.cloned.1.call-update) | async-done | bytes 294928 | tf_op jit(solution)/shard_map/reduce_scatter | solution.py:297
  843.9 46.1 %reduce-scatter.32.cloned.1.call-done = f32[96,768]{1,0:T(8,128)} async-done(((f32[768,768]{1,0:T(8,128)}), f32[96,768]{1,0:T(8,128)}) %reduce-scatter.32.cloned.1.call-update) | async-done | bytes 294928 | tf_op jit(solution)/shard_map/reduce_scatter | solution.py:295
  (500 shorter events, 191.4 us)
Async XLA Ops:
  8.0 27.0 %copy-start = (bf16[2,512,768]{2,1,0:T(8,128)(2,1)S(1)}, bf16[2,512,768]{2,1,0:T(8,128)(2,1)}, u32[]{:S(2)}) copy-start(bf16[2,512,768]{2,1,0:T(8,128)(2,1)} %param.12) | copy-start | bytes 4718596
  8.0 271.8 %all-reduce.16.cloned.1.call-start = ((), (), s32[]{:S(2)}) async-start(), calls=%async_computation.26 | async-start | bytes 6291456 | tf_op jit(solution)/shard_map/psum | solution.py:111
  33.3 15.8 %copy-start.75 = (bf16[3,96,192]{2,1,0:T(8,128)(2,1)S(1)}, bf16[3,96,192]{2,1,0:T(8,128)(2,1)}, u32[]{:S(2)}) copy-start(bf16[3,96,192]{2,1,0:T(8,128)(2,1)} %param.14) | copy-start | bytes 331780
  35.0 40.7 %copy-start.90 = (f32[512]{0:T(512)}, f32[512]{0:T(512)S(1)}, u32[]{:S(2)}) copy-start(f32[512]{0:T(512)S(1)} %get-tuple-element.168) | copy-start | bytes 6148
  35.0 42.9 %copy-start.92 = (f32[512]{0:T(512)}, f32[512]{0:T(512)S(1)}, u32[]{:S(2)}) copy-start(f32[512]{0:T(512)S(1)} %get-tuple-element.169) | copy-start | bytes 6148
  35.6 39.5 %copy-start.110 = (f32[512]{0:T(512)}, f32[512]{0:T(512)S(1)}, u32[]{:S(2)}) copy-start(f32[512]{0:T(512)S(1)} %get-tuple-element.87) | copy-start | bytes 6148
  36.2 41.6 %copy-start.105 = (f32[512]{0:T(512)}, f32[512]{0:T(512)S(1)}, u32[]{:S(2)}) copy-start(f32[512]{0:T(512)S(1)} %fusion.151) | copy-start | bytes 6148
  36.2 39.5 %copy-start.107 = (f32[512]{0:T(512)}, f32[512]{0:T(512)S(1)}, u32[]{:S(2)}) copy-start(f32[512]{0:T(512)S(1)} %fusion.153) | copy-start | bytes 6148
  90.3 17.6 %copy-start.64 = (bf16[512,192]{0,1:T(8,128)(2,1)}, bf16[512,192]{0,1:T(8,128)(2,1)S(1)}, u32[]{:S(2)}) copy-start(bf16[512,192]{0,1:T(8,128)(2,1)S(1)} %get-tuple-element.126) | copy-start | bytes 589828
  107.9 17.8 %copy-start.63 = (bf16[512,192]{0,1:T(8,128)(2,1)S(1)}, bf16[512,192]{0,1:T(8,128)(2,1)}, u32[]{:S(2)}) copy-start(bf16[512,192]{0,1:T(8,128)(2,1)} %get-tuple-element.127) | copy-start | bytes 589828
  108.0 26.0 %copy-start.62 = (bf16[512,192]{0,1:T(8,128)(2,1)S(1)}, bf16[512,192]{0,1:T(8,128)(2,1)}, u32[]{:S(2)}) copy-start(bf16[512,192]{0,1:T(8,128)(2,1)} %get-tuple-element.138) | copy-start | bytes 589828
  125.7 18.6 %copy-start.14 = (f32[512,1024]{1,0:T(8,128)S(1)}, f32[512,1024]{1,0:T(8,128)}, u32[]{:S(2)}) copy-start(f32[512,1024]{1,0:T(8,128)} %get-tuple-element.149) | copy-start | bytes 6291460
  134.0 20.2 %copy-start.38 = (bf16[1024,192]{0,1:T(8,128)(2,1)}, bf16[1024,192]{0,1:T(8,128)(2,1)S(1)}, u32[]{:S(2)}) copy-start(bf16[1024,192]{0,1:T(8,128)(2,1)S(1)} %all_gather.74) | copy-start | bytes 1179652
  158.0 126.5 %all-gather.8.cloned.1.call-start = ((), (), s32[]{:S(2)}) async-start(), calls=%async_computation.11 | async-start | bytes 1327104 | tf_op jit(solution)/shard_map/all_gather | solution.py:61
  158.6 132.0 %all-gather.10.cloned.1.call-start = ((), (), s32[]{:S(2)}) async-start(), calls=%async_computation.12 | async-start | bytes 1327104 | tf_op jit(solution)/shard_map/all_gather | solution.py:63
  159.2 263.0 %all-reduce.14.cloned.1.call-start = ((), (), s32[]{:S(2)}) async-start(), calls=%async_computation.25 | async-start | bytes 6291456 | tf_op jit(solution)/shard_map/psum | solution.py:207
  282.2 140.0 %copy-start.19 = (f32[512,768]{1,0:T(8,128)}, f32[512,768]{1,0:T(8,128)S(1)}, u32[]{:S(2)}) copy-start(f32[512,768]{1,0:T(8,128)S(1)} %get-tuple-element.121) | copy-start | bytes 4718596
  282.2 210.9 %copy-start.97 = (f32[512]{0:T(512)}, f32[512]{0:T(512)S(1)}, u32[]{:S(2)}) copy-start(f32[512]{0:T(512)S(1)} %broadcast_multiply_fusion) | copy-start | bytes 6148
  301.5 191.6 %all-reduce.18.cloned.1.call-start = ((), (), s32[]{:S(2)}) async-start(), calls=%async_computation.27 | async-start | bytes 3145728 | tf_op jit(solution)/shard_map/psum | solution.py:120
  307.5 254.6 %reduce-scatter.26.cloned.1.call-start = ((), (), s32[]{:S(2)}) async-start(), calls=%async_computation.14 | async-start | bytes 1179648 | tf_op jit(solution)/shard_map/reduce_scatter | solution.py:267
  516.0 47.7 %reduce-scatter.30.cloned.1.call-start = ((), (), s32[]{:S(2)}) async-start(), calls=%async_computation.16 | async-start | bytes 1179648 | tf_op jit(solution)/shard_map/reduce_scatter | solution.py:267
  530.5 41.5 %reduce-scatter.24.cloned.1.call-start = ((), (), s32[]{:S(2)}) async-start(), calls=%async_computation.13 | async-start | bytes 1179648 | tf_op jit(solution)/shard_map/reduce_scatter | solution.py:266
  542.8 48.8 %reduce-scatter.28.cloned.1.call-start = ((), (), s32[]{:S(2)}) async-start(), calls=%async_computation.15 | async-start | bytes 1179648 | tf_op jit(solution)/shard_map/reduce_scatter | solution.py:266
  557.9 160.4 %all-reduce.12.cloned.1.call-start = ((), (), s32[]{:S(2)}) async-start(), calls=%async_computation.24 | async-start | bytes 6291456 | tf_op jit(solution)/shard_map/psum | solution.py:277
  596.7 149.9 %reduce-scatter.44.cloned.1.call-start = ((), (), s32[]{:S(2)}) async-start(), calls=%async_computation.23 | async-start | bytes 442368
  605.3 142.7 %reduce-scatter.38.cloned.1.call-start = ((), (), s32[]{:S(2)}) async-start(), calls=%async_computation.20 | async-start | bytes 884736
  610.3 167.6 %reduce-scatter.36.cloned.1.call-start = ((), (), s32[]{:S(2)}) async-start(), calls=%async_computation.19 | async-start | bytes 2211840
  623.5 162.7 %reduce-scatter.40.cloned.1.call-start = ((), (), s32[]{:S(2)}) async-start(), calls=%async_computation.21 | async-start | bytes 442368
  727.1 70.1 %reduce-scatter.42.cloned.1.call-start = ((), (), s32[]{:S(2)}) async-start(), calls=%async_computation.22 | async-start | bytes 442368
  730.2 113.7 %reduce-scatter.34.cloned.1.call-start = ((), (), s32[]{:S(2)}) async-start(), calls=%async_computation.18 | async-start | bytes 2654208 | tf_op jit(solution)/shard_map/reduce_scatter | solution.py:297
  735.1 154.9 %reduce-scatter.32.cloned.1.call-start = ((), (), s32[]{:S(2)}) async-start(), calls=%async_computation.17 | async-start | bytes 2654208 | tf_op jit(solution)/shard_map/reduce_scatter | solution.py:295
  746.5 34.7 %copy-start.94 = (f32[512]{0:T(512)S(1)}, f32[512]{0:T(512)}, u32[]{:S(2)}) copy-start(f32[512]{0:T(512)} %copy-done.92) | copy-start | bytes 6148
  (124 other events, 387.0 us)
Sparse Core Ops, SparseCore 0:
  158.1 121.6 all-reduce.15
  301.6 120.4 all-reduce.13
  424.5 68.4 all-reduce.17
  596.8 121.4 all-reduce.11
Sparse Core Ops, SparseCore 1:
  160.3 24.1 all-gather.7
  186.3 23.8 all-gather.9
  516.1 16.4 reduce-scatter.25
  534.9 17.3 reduce-scatter.29
  554.5 17.4 reduce-scatter.23
  574.3 17.2 reduce-scatter.27
  605.4 34.0 reduce-scatter.43
  642.5 34.9 reduce-scatter.37
  680.7 40.1 reduce-scatter.35
  727.2 32.8 reduce-scatter.39
  763.3 33.8 reduce-scatter.41
  801.5 42.3 reduce-scatter.33
  847.7 42.3 reduce-scatter.31
where the time goes:
time: 906 us; the launch traced here: 898 us
  waiting for transfers between devices  484 us (53%)
  blocking collectives  160 us (18%)
  matrix products  112 us (12%)
  other arithmetic  67.5 us (7%)
  local copies, waits for them, and re-layouts  55.2 us (6%)
  between operations  17.9 us (2%)
    psum x1, waiting for transfers between devices, per_device(): lax.psum(jnp.einsum('cf,df->cd', grad_pre, upward_full, preferred_element...  114 us
    psum x1, waiting for transfers between devices, per_device(): lax.psum(jnp.dot(attended, mixer_weights, preferred_element_type=jnp.floa...  91.5 us
    psum x1, waiting for transfers between devices, per_device(): lax.psum(jnp.einsum('tce,tde->cd', triple, entry_weights, preferred_eleme...  88.1 us
    psum x1, waiting for transfers between devices, per_device(): lax.psum(jnp.dot(activated, downward_full, preferred_element_type=jnp.flo...  66.1 us
    reduce_scatter x1, waiting for transfers between devices, per_device(): lax.psum_scatter(upward_acc, ('dp', 'seq'), scatter_dimension=0, tiled=True)  46.1 us
    unnamed x298, local copies, waits for them, and re-layouts  46 us
    reduce_scatter x1, waiting for transfers between devices, per_device(): lax.psum_scatter(downward_acc, ('dp', 'seq'), scatter_dimension=1, tiled=...  45.3 us
    unnamed x1, blocking collectives  24.1 us
  transfers between devices with their start and end apart: 17, of which 9 were waited for; matrix products, arithmetic and copies ran while one was open for 17% of the time, Pallas kernels for 0%

commit v1 on v0

--- a/solution.py
+++ b/solution.py
@@ -1,7 +1,35 @@
+import functools
 import jax
 import jax.numpy as jnp
 from jax import lax
 from jax.sharding import PartitionSpec as P
+from jax.lax import axis_index, axis_size, ppermute
+
+
+def mix_record(page, pos_dim):
+    raw_out = axis_index(("dp", "seq"))
+    w2 = axis_size(("dp", "seq"))
+    mat_out, t1, inter = (w2, raw_out, page.shape[pos_dim])
+    k0 = 0
+    slots = []
+    while k0 < mat_out:
+        slots.append((k0, (k0 + 1) % mat_out))
+        k0 += 1
+    shaped = jnp.zeros(
+        (*page.shape[:pos_dim], mat_out * inter, *page.shape[pos_dim + 1 :]), page.dtype
+    )
+    y2 = page
+    k = 0
+    while k < mat_out:
+        y = (t1 - k) % mat_out
+        shaped = lax.dynamic_update_slice_in_dim(shaped, y2, y * inter, axis=pos_dim)
+        if k < mat_out - 1:
+            y2 = ppermute(y2, axis_name=("dp", "seq"), perm=slots)
+        k += 1
+    return shaped
+
+
+solve_sector = functools.partial(mix_record, pos_dim=1)
 
 
 def norm_rows(values, gain_row, shift_row):
@@ -55,7 +83,7 @@
     results = []
     for batch_index in range(micro):
         gathered = (
-            lax.all_gather(projections, ("dp", "seq"), axis=1, tiled=True),
+            solve_sector(projections),
             lax.all_gather(offsets, ("dp", "seq"), axis=2, tiled=True),
             lax.all_gather(mixing, ("dp", "seq"), axis=1, tiled=True),
             lax.all_gather(upward, ("dp", "seq"), axis=0, tiled=True),

time: 906 us -> 893 us (0.986)
  starting transfers between devices: 1.52 us -> 13.3 us
    psum x1, waiting for transfers between devices: 114 us -> 91.5 us  [per_device(): lax.psum(jnp.einsum('cf,df->cd', grad_pre, upward_full, preferred_element...]
    ppermute x0 -> x7, waiting for transfers between devices: none -> 15.6 us  [mix_record(): y2 = ppermute(y2, axis_name=('dp', 'seq'), perm=slots)]
    ppermute x0 -> x7, starting transfers between devices: none -> 12.1 us  [mix_record(): y2 = ppermute(y2, axis_name=('dp', 'seq'), perm=slots)]
  transfers between devices with their start and end apart: 17 -> 24, of which waited for: 9 -> 13; matrix products, arithmetic and copies ran while one was open for 17% -> 18% of each run, Pallas kernels for 0% -> 0%
where the time goes in v1:
time: 893 us; the launch traced here: 887 us
  waiting for transfers between devices  476 us (53%)
  blocking collectives  154 us (17%)
  matrix products  103 us (12%)
  other arithmetic  63.9 us (7%)
  local copies, waits for them, and re-layouts  59.1 us (7%)
  between operations  18.3 us (2%)
  starting transfers between devices  13.3 us (1%)
    psum x1, waiting for transfers between devices, per_device(): lax.psum(jnp.einsum('cf,df->cd', grad_pre, upward_full, preferred_element...  91.5 us
    psum x1, waiting for transfers between devices, per_device(): lax.psum(jnp.dot(attended, mixer_weights, preferred_element_type=jnp.floa...  90.7 us
    psum x1, waiting for transfers between devices, per_device(): lax.psum(jnp.einsum('tce,tde->cd', triple, entry_weights, preferred_eleme...  88 us
    psum x1, waiting for transfers between devices, per_device(): lax.psum(jnp.dot(activated, downward_full, preferred_element_type=jnp.flo...  66.1 us
    reduce_scatter x1, waiting for transfers between devices, per_device(): lax.psum_scatter(upward_acc, ('dp', 'seq'), scatter_dimension=0, tiled=True)  46.1 us
    reduce_scatter x1, waiting for transfers between devices, per_device(): lax.psum_scatter(downward_acc, ('dp', 'seq'), scatter_dimension=1, tiled=...  45.2 us
    unnamed x298, local copies, waits for them, and re-layouts  40 us
    unnamed x1, blocking collectives  24.1 us
  transfers between devices with their start and end apart: 24, of which 13 were waited for; matrix products, arithmetic and copies ran while one was open for 18% of the time, Pallas kernels for 0%

profile of v1, /device:TPU:0, one launch (start us, length us, event | category | flops | bytes accessed | tf_op | source)
XLA Modules:
  0.0 887.5 jit_solution(17064295953588478702)
XLA Ops:
  11.9 11.4 %all-gather.2 = bf16[8,96,2]{1,2,0:T(2,128)(2,1)S(1)} all-gather(bf16[1,96,2]{1,2,0:T(2,128)(2,1)} %bitcast.295), channel_id=1, replica_groups=mesh['dp'=4,'seq'=2,'tensor'=4] {'dp','seq'}, dimensions={0}, use_global_device_ids=true | all-gather | bytes 3456 | tf_op jit(solution)/shard_map/all_gather | solution.py:92
  23.3 10.9 %all-gather.3 = bf16[8,96,2]{1,2,0:T(2,128)(2,1)S(1)} all-gather(bf16[1,96,2]{1,2,0:T(2,128)(2,1)} %bitcast.296), channel_id=1, replica_groups=mesh['dp'=4,'seq'=2,'tensor'=4] {'dp','seq'}, dimensions={0}, use_global_device_ids=true | all-gather | bytes 3456 | tf_op jit(solution)/shard_map/all_gather | solution.py:93
  35.9 12.5 %all_gather.28 = bf16[2,3,64]{1,0,2:T(2,128)(2,1)S(1)} all-gather(bf16[2,3,8]{1,0,2:T(2,128)(2,1)S(1)} %copy.95), channel_id=1, replica_groups=mesh['dp'=4,'seq'=2,'tensor'=4] {'dp','seq'}, dimensions={2}, use_global_device_ids=true | all-gather | bytes 864 | tf_op jit(solution)/shard_map/all_gather | solution.py:87
  51.6 17.5 %all_gather.31 = bf16[192,768]{0,1:T(8,128)(2,1)S(1)} all-gather(bf16[192,96]{0,1:T(8,128)(2,1)S(1)} %copy.98), channel_id=1, replica_groups=mesh['dp'=4,'seq'=2,'tensor'=4] {'dp','seq'}, dimensions={1}, use_global_device_ids=true | all-gather | bytes 331776 | tf_op jit(solution)/shard_map/all_gather | solution.py:88
  69.9 4.9 collective-permute-done.2
  87.7 3.9 collective-permute-done.5
  106.7 6.4 all-gather
  115.5 6.6 all-gather.1
  124.4 7.6 all_gather.71
  132.0 6.3 all_gather.30
  149.3 11.4 %all-gather.4 = bf16[8,96,2]{1,2,0:T(2,128)(2,1)S(1)} all-gather(bf16[1,96,2]{1,2,0:T(2,128)(2,1)S(1)} %bitcast.297), channel_id=1, replica_groups=mesh['dp'=4,'seq'=2,'tensor'=4] {'dp','seq'}, dimensions={0}, use_global_device_ids=true | all-gather | bytes 3456 | tf_op jit(solution)/shard_map/all_gather | solution.py:94
  161.4 16.5 %all_gather.68 = bf16[12,64]{0,1:T(8,128)(2,1)S(1)} all-gather(bf16[12,8]{0,1:T(8,128)(2,1)S(1)} %copy-done.131), channel_id=1, replica_groups=mesh['dp'=4,'seq'=2,'tensor'=4] {'dp','seq'}, dimensions={1}, use_global_device_ids=true | all-gather | bytes 1728 | tf_op jit(solution)/shard_map/all_gather | solution.py:90
  178.6 90.7 %all-reduce.16.cloned.1.call-done = (f32[512,768]{1,0:T(8,128)}, f32[512,768]{1,0:T(8,128)}) async-done(((f32[512,768]{1,0:T(8,128)}, f32[512,768]{1,0:T(8,128)}), (f32[512,768]{1,0:T(8,128)}, f32[512,768]{1,0:T(8,128)})) %all-reduce.16.cloned.1.call-update) | async-done | bytes 3145744 | tf_op jit(solution)/shard_map/psum | solution.py:139
  274.1 3.9 convolution_add_fusion.3
  280.2 4.5 convert_reduce_fusion.5
  291.2 3.9 convolution_convert_fusion.1
  297.1 23.1 %all_gather.72 = bf16[3,768,192]{2,1,0:T(8,128)(2,1)} all-gather(bf16[3,96,192]{2,1,0:T(8,128)(2,1)} %param.14), channel_id=1, replica_groups=mesh['dp'=4,'seq'=2,'tensor'=4] {'dp','seq'}, dimensions={1}, use_global_device_ids=true | all-gather | bytes 995328 | tf_op jit(solution)/shard_map/all_gather | solution.py:183
  320.2 91.5 %all-reduce.14.cloned.1.call-done = (f32[512,768]{1,0:T(8,128)}, f32[512,768]{1,0:T(8,128)}) async-done(((f32[512,768]{1,0:T(8,128)}, f32[512,768]{1,0:T(8,128)}), (f32[512,768]{1,0:T(8,128)}, f32[512,768]{1,0:T(8,128)})) %all-reduce.14.cloned.1.call-update) | async-done | bytes 3145744 | tf_op jit(solution)/shard_map/psum | solution.py:235
  416.6 66.1 %all-reduce.18.cloned.1.call-done = (bf16[512,768]{1,0:T(8,128)(2,1)}, bf16[512,768]{1,0:T(8,128)(2,1)}) async-done(((bf16[512,768]{1,0:T(8,128)(2,1)}, bf16[512,768]{1,0:T(8,128)(2,1)}), (bf16[512,768]{1,0:T(8,128)(2,1)}, bf16[512,768]{1,0:T(8,128)(2,1)})) %all-reduce.18.cloned.1.call-update) | async-done | bytes 1572880 | tf_op jit(solution)/shard_map/psum | solution.py:148
  482.7 5.0 fusion.181
  554.9 6.7 reduce-scatter.24.cloned.1.call-done
  566.7 14.6 %reduce-scatter.28.cloned.1.call-done = f32[512,192]{0,1:T(8,128)} async-done(((f32[1024,192]{0,1:T(8,128)}), f32[512,192]{0,1:T(8,128)}) %reduce-scatter.28.cloned.1.call-update) | async-done | bytes 393232 | tf_op jit(solution)/shard_map/reduce_scatter | solution.py:294
  604.3 4.2 copy.104
  608.5 4.7 reshape.314
  613.6 4.1 fusion.65
  620.0 88.0 %all-reduce.12.cloned.1.call-done = (f32[512,768]{1,0:T(8,128)}, f32[512,768]{1,0:T(8,128)}) async-done(((f32[512,768]{1,0:T(8,128)}, f32[512,768]{1,0:T(8,128)}), (f32[512,768]{1,0:T(8,128)}, f32[512,768]{1,0:T(8,128)})) %all-reduce.12.cloned.1.call-update) | async-done | bytes 3145744 | tf_op jit(solution)/shard_map/psum | solution.py:305
  720.0 4.9 convolution_add_fusion
  742.1 24.1 %all-reduce.2 = (f32[2,3,64]{2,1,0:T(4,128)S(1)}, f32[12,64]{1,0:T(8,128)S(1)}) all-reduce(f32[2,3,64]{2,1,0:T(4,128)S(1)} %maximum_add_fusion.3, f32[12,64]{1,0:T(8,128)} %add.493), channel_id=9, replica_groups=mesh['dp'=4,'seq'=2,'tensor'=4] {'dp','seq'}, use_global_device_ids=true, to_apply=%region_49.50.clone | all-reduce | flops 1152 | bytes 9216
  770.9 3.7 fusion.56
  777.3 9.7 %reduce-scatter.42.cloned.1.call-done = f32[96,2]{1,0:T(8,128)} async-done(((f32[768,2]{1,0:T(8,128)}), f32[96,2]{1,0:T(8,128)}) %reduce-scatter.42.cloned.1.call-update) | async-done | bytes 784
  788.5 45.2 %reduce-scatter.34.cloned.1.call-done = f32[768,96]{0,1:T(8,128)} async-done(((f32[768,768]{0,1:T(8,128)}), f32[768,96]{0,1:T(8,128)}) %reduce-scatter.34.cloned.1.call-update) | async-done | bytes 294928 | tf_op jit(solution)/shard_map/reduce_scatter | solution.py:325
  833.7 46.1 %reduce-scatter.32.cloned.1.call-done = f32[96,768]{1,0:T(8,128)} async-done(((f32[768,768]{1,0:T(8,128)}), f32[96,768]{1,0:T(8,128)}) %reduce-scatter.32.cloned.1.call-update) | async-done | bytes 294928 | tf_op jit(solution)/shard_map/reduce_scatter | solution.py:323
  (530 shorter events, 208.6 us)
Async XLA Ops:
  8.0 40.5 %copy-start = (bf16[2,512,768]{2,1,0:T(8,128)(2,1)S(1)}, bf16[2,512,768]{2,1,0:T(8,128)(2,1)}, u32[]{:S(2)}) copy-start(bf16[2,512,768]{2,1,0:T(8,128)(2,1)} %param.12) | copy-start | bytes 4718596
  8.0 261.3 %all-reduce.16.cloned.1.call-start = ((), (), s32[]{:S(2)}) async-start(), calls=%async_computation.26 | async-start | bytes 6291456 | tf_op jit(solution)/shard_map/psum | solution.py:139
  8.1 41.1 %collective-permute-start = (bf16[3,96,192]{2,1,0:T(8,128)(2,1)}, bf16[3,96,192]{2,1,0:T(8,128)(2,1)S(1)}, u32[]{:S(2)}, u32[]{:S(2)}) collective-permute-start(bf16[3,96,192]{2,1,0:T(8,128)(2,1)} %param.14), channel_id=1, source_target_pairs={{0,4},{4,8},{8,12},{12,16},{16,20},{20,24},{24,28},{28,0},{1,5},{5... | collective-permute-start | bytes 331784 | tf_op jit(solution)/shard_map/ppermute | solution.py:27
  48.5 56.4 %copy-start.90 = (f32[512]{0:T(512)}, f32[512]{0:T(512)S(1)}, u32[]{:S(2)}) copy-start(f32[512]{0:T(512)S(1)} %get-tuple-element.168) | copy-start | bytes 6148
  48.5 57.3 %copy-start.92 = (f32[512]{0:T(512)}, f32[512]{0:T(512)S(1)}, u32[]{:S(2)}) copy-start(f32[512]{0:T(512)S(1)} %get-tuple-element.169) | copy-start | bytes 6148
  49.1 56.6 %copy-start.105 = (f32[512]{0:T(512)}, f32[512]{0:T(512)S(1)}, u32[]{:S(2)}) copy-start(f32[512]{0:T(512)S(1)} %fusion.150) | copy-start | bytes 6148
  49.2 20.0 %collective-permute-start.1 = (bf16[3,96,192]{2,1,0:T(8,128)(2,1)S(1)}, bf16[3,96,192]{2,1,0:T(8,128)(2,1)S(1)}, u32[]{:S(2)}, u32[]{:S(2)}) collective-permute-start(bf16[3,96,192]{2,1,0:T(8,128)(2,1)S(1)} %collective-permute-done), channel_id=1, source_target_pairs={{0,4},{4,8},{8,12},{12,16},{16,20},{20,24},{24,28},{28,0},{1,5},{5... | collective-permute-start | bytes 331784 | tf_op jit(solution)/shard_map/ppermute | solution.py:27
  50.1 54.7 %copy-start.107 = (f32[512]{0:T(512)}, f32[512]{0:T(512)S(1)}, u32[]{:S(2)}) copy-start(f32[512]{0:T(512)S(1)} %fusion.152) | copy-start | bytes 6148
  69.1 5.6 collective-permute-start.2
  74.7 5.6 collective-permute-start.3
  80.3 5.6 collective-permute-start.4
  85.9 5.7 collective-permute-start.5
  91.6 10.9 %collective-permute-start.6 = (bf16[3,96,192]{2,1,0:T(8,128)(2,1)}, bf16[3,96,192]{2,1,0:T(8,128)(2,1)}, u32[]{:S(2)}, u32[]{:S(2)}) collective-permute-start(bf16[3,96,192]{2,1,0:T(8,128)(2,1)} %collective-permute-done.5), channel_id=1, source_target_pairs={{0,4},{4,8},{8,12},{12,16},{16,20},{20,24},{24,28},{28,0},{1,5},{5... | collective-permute-start | bytes 331784 | tf_op jit(solution)/shard_map/ppermute | solution.py:27
  148.1 126.0 %all-gather.8.cloned.1.call-start = ((), (), s32[]{:S(2)}) async-start(), calls=%async_computation.11 | async-start | bytes 1327104 | tf_op jit(solution)/shard_map/all_gather | solution.py:89
  148.7 131.5 %all-gather.10.cloned.1.call-start = ((), (), s32[]{:S(2)}) async-start(), calls=%async_computation.12 | async-start | bytes 1327104 | tf_op jit(solution)/shard_map/all_gather | solution.py:91
  149.3 262.5 %all-reduce.14.cloned.1.call-start = ((), (), s32[]{:S(2)}) async-start(), calls=%async_computation.25 | async-start | bytes 6291456 | tf_op jit(solution)/shard_map/psum | solution.py:235
  271.7 140.0 %copy-start.19 = (f32[512,768]{1,0:T(8,128)}, f32[512,768]{1,0:T(8,128)S(1)}, u32[]{:S(2)}) copy-start(f32[512,768]{1,0:T(8,128)S(1)} %get-tuple-element.121) | copy-start | bytes 4718596
  271.8 210.9 %copy-start.97 = (f32[512]{0:T(512)}, f32[512]{0:T(512)S(1)}, u32[]{:S(2)}) copy-start(f32[512]{0:T(512)S(1)} %broadcast_multiply_fusion) | copy-start | bytes 6148
  291.2 191.6 %all-reduce.18.cloned.1.call-start = ((), (), s32[]{:S(2)}) async-start(), calls=%async_computation.27 | async-start | bytes 3145728 | tf_op jit(solution)/shard_map/psum | solution.py:148
  297.1 254.4 %reduce-scatter.26.cloned.1.call-start = ((), (), s32[]{:S(2)}) async-start(), calls=%async_computation.14 | async-start | bytes 1179648 | tf_op jit(solution)/shard_map/reduce_scatter | solution.py:295
  505.7 47.5 %reduce-scatter.30.cloned.1.call-start = ((), (), s32[]{:S(2)}) async-start(), calls=%async_computation.16 | async-start | bytes 1179648 | tf_op jit(solution)/shard_map/reduce_scatter | solution.py:295
  520.3 41.3 %reduce-scatter.24.cloned.1.call-start = ((), (), s32[]{:S(2)}) async-start(), calls=%async_computation.13 | async-start | bytes 1179648 | tf_op jit(solution)/shard_map/reduce_scatter | solution.py:294
  532.5 48.8 %reduce-scatter.28.cloned.1.call-start = ((), (), s32[]{:S(2)}) async-start(), calls=%async_computation.15 | async-start | bytes 1179648 | tf_op jit(solution)/shard_map/reduce_scatter | solution.py:294
  547.4 160.6 %all-reduce.12.cloned.1.call-start = ((), (), s32[]{:S(2)}) async-start(), calls=%async_computation.24 | async-start | bytes 6291456 | tf_op jit(solution)/shard_map/psum | solution.py:305
  586.4 149.8 %reduce-scatter.44.cloned.1.call-start = ((), (), s32[]{:S(2)}) async-start(), calls=%async_computation.23 | async-start | bytes 442368
  595.1 142.6 %reduce-scatter.38.cloned.1.call-start = ((), (), s32[]{:S(2)}) async-start(), calls=%async_computation.20 | async-start | bytes 884736
  600.1 167.5 %reduce-scatter.36.cloned.1.call-start = ((), (), s32[]{:S(2)}) async-start(), calls=%async_computation.19 | async-start | bytes 2211840
  613.3 162.6 %reduce-scatter.40.cloned.1.call-start = ((), (), s32[]{:S(2)}) async-start(), calls=%async_computation.21 | async-start | bytes 442368
  716.9 70.1 %reduce-scatter.42.cloned.1.call-start = ((), (), s32[]{:S(2)}) async-start(), calls=%async_computation.22 | async-start | bytes 442368
  719.9 113.7 %reduce-scatter.34.cloned.1.call-start = ((), (), s32[]{:S(2)}) async-start(), calls=%async_computation.18 | async-start | bytes 2654208 | tf_op jit(solution)/shard_map/reduce_scatter | solution.py:325
  724.9 154.9 %reduce-scatter.32.cloned.1.call-start = ((), (), s32[]{:S(2)}) async-start(), calls=%async_computation.17 | async-start | bytes 2654208 | tf_op jit(solution)/shard_map/reduce_scatter | solution.py:323
  736.2 34.7 %copy-start.94 = (f32[512]{0:T(512)S(1)}, f32[512]{0:T(512)}, u32[]{:S(2)}) copy-start(f32[512]{0:T(512)} %copy-done.92) | copy-start | bytes 6148
  (131 other events, 621.2 us)
Sparse Core Ops, SparseCore 0:
  148.2 121.0 all-reduce.15
  291.3 120.4 all-reduce.13
  414.2 68.4 all-reduce.17
  586.5 121.4 all-reduce.11
Sparse Core Ops, SparseCore 1:
  150.5 23.5 all-gather.7
  175.8 23.9 all-gather.9
  505.8 16.4 reduce-scatter.25
  524.6 17.3 reduce-scatter.29
  544.2 17.3 reduce-scatter.23
  563.9 17.3 reduce-scatter.27
  595.1 34.0 reduce-scatter.43
  632.3 35.0 reduce-scatter.37
  670.6 40.1 reduce-scatter.35
  717.0 32.8 reduce-scatter.39
  753.1 33.8 reduce-scatter.41
  791.3 42.3 reduce-scatter.33
  837.5 42.3 reduce-scatter.31
